TPU v7x, 32 devices: a whole 2x2x4 slice. The times are simulated.
32 devices in a mesh: groups: 2 (over x), dp: 16 (over z, y, core).
Axes of the slice: x: 2, y: 2, z: 4, core: 2. Of those that a mesh axis runs over, the one named last changes fastest.
Arguments:
- inputs: bfloat16 [8192, 4096], P(('groups', 'dp')), parts along dimension 0, may hold values from -6 to 6
- gate_values: bfloat16 [8192, 4096], P(('groups', 'dp')), parts along dimension 0, may hold values from -6 to 6
- write_proj: bfloat16 [8192, 128], P(('groups', 'dp')), parts along dimension 0, may hold values from -6 to 6
- read_proj: bfloat16 [8192, 128], P(('groups', 'dp')), parts along dimension 0, may hold values from -0.59765625 to 0.59765625
- step_raw: bfloat16 [8192, 64], P(('groups', 'dp')), parts along dimension 0, may hold values from -3 to 10
- cotangent: bfloat16 [8192, 4096], P(('groups', 'dp')), parts along dimension 0, may hold values from -6 to 6
- step_bias: float32 [64], replicated, may hold values from -5.5 to -3.5
- rate_log: float32 [64], replicated
- skip_gain: float32 [64], replicated, may hold values from 0.5 to 1.5
- norm_gain: float32 [4096], replicated, may hold values from 0.5 to 1.5
- state_bank: bfloat16 [128, 64, 64, 128], P('groups', 'dp'), parts along dimension 0, may hold values from -1.796875 to 1.796875
- turn_index: int32 [8192], P(('groups', 'dp')), parts along dimension 0, may hold values from 0 to 3, as said below
- turn_slot: int32 [128], P('groups'), parts along dimension 0, may hold values from 0 to 63, each once
Outputs:
- grad_inputs: bfloat16 [8192, 4096], P(('groups', 'dp')), parts along dimension 0
- state_grad: bfloat16 [128, 64, 64, 128], P('groups', 'dp'), parts along dimension 0
- gain_grad: float32 [8192], P(('groups', 'dp')), parts along dimension 0
- head_grads: float32 [6, 64], P('groups'), parts along dimension 0
There are 2 independent parts, one for each index of `groups`. A program takes and returns all parts, laid end to end along the dimension named above; an argument that names none is the same for every part. Nothing has to cross between parts.
Inputs may be any that keep to these rules, and one draw needn't show every extreme that they name: `turn_index`: within each device's 256 tokens turn numbers start at 0, never fall and rise by one at each new turn; some device has 4 turns. `turn_slot`: each slot number appears once.
All inputs are finite; a program needn't handle non-finite values.
Results may differ from a plain program's by a relative error of at most 0.0051.
Values may be sent and summed in bfloat16 or wider, within the bound.
No kernel may reach another device: no remote copies, remote signals or barrier semaphores. Data moves between devices by JAX's collectives and lax.ppermute only.
A program may use at most 128 MiB of HBM per device.

v0:
```python
import jax
import jax.numpy as jnp
from jax import lax
from jax.sharding import PartitionSpec as P

HDIM = 64
DSTATE = 128
BLOCK_LEN = 256
TMAX = 4


def project_turns(states, read_proj, turn_index):
    turn_cap = states.shape[0]
    onehot = turn_index[:, None] == jnp.arange(turn_cap, dtype=jnp.int32)[None, :]
    masked = jnp.where(onehot[:, :, None], read_proj[:, None, :], jnp.zeros((), read_proj.dtype))
    return jnp.einsum("tgn,ghpn->thp", masked, states, preferred_element_type=jnp.float32).astype(
        jnp.bfloat16
    )


def turn_grads(read_grad, read_proj, turn_index, turn_cap):
    onehot = turn_index[:, None] == jnp.arange(turn_cap, dtype=jnp.int32)[None, :]
    masked = jnp.where(onehot[:, :, None], read_proj[:, None, :], jnp.zeros((), read_proj.dtype))
    return jnp.einsum("tgn,thp->ghpn", masked, read_grad, preferred_element_type=jnp.float32)


def mixer(
    input_value,
    start_read,
    bias_value,
    rate_value,
    skip_value,
    gain_value,
    gate_values,
    write_proj,
    read_proj,
    step_raw,
    turn_index,
):
    row_count = input_value.shape[0]
    head_count = step_raw.shape[1]
    head_dim = input_value.shape[1] // head_count
    state_dim = write_proj.shape[1]
    block_count = row_count // BLOCK_LEN
    highest = lax.Precision.HIGHEST
    step_size = jax.nn.softplus(step_raw.astype(jnp.float32) + bias_value[None, :])
    log_decay = -jnp.exp(rate_value)[None, :] * step_size
    starts = jnp.concatenate([jnp.ones((1,), jnp.bool_), turn_index[1:] != turn_index[:-1]])
    blocked = (
        input_value.reshape(block_count, BLOCK_LEN, head_count, head_dim),
        write_proj.reshape(block_count, BLOCK_LEN, state_dim),
        read_proj.reshape(block_count, BLOCK_LEN, state_dim),
        step_size.reshape(block_count, BLOCK_LEN, head_count),
        log_decay.reshape(block_count, BLOCK_LEN, head_count),
        turn_index.reshape(block_count, BLOCK_LEN),
        starts.reshape(block_count, BLOCK_LEN),
        start_read.reshape(block_count, BLOCK_LEN, head_count, head_dim),
    )
    token_positions = jnp.arange(BLOCK_LEN, dtype=jnp.int32)
    causal_mask = token_positions[:, None] >= token_positions[None, :]

    def advance(carried, pieces):
        state_now, since_now = carried
        (
            block_x,
            block_write,
            block_read,
            block_step,
            block_decay,
            block_turn,
            block_start,
            block_begin,
        ) = pieces
        running = jnp.cumsum(block_decay, axis=0)
        before = running - block_decay
        same_mask = (causal_mask & (block_turn[:, None] == block_turn[None, :]))[:, :, None]
        decay_mat = jnp.exp(jnp.where(same_mask, running[:, None, :] - running[None, :, :], -1e30))
        offset = jnp.max(jnp.where(same_mask, before[None, :, :], -1e30), axis=1)
        scores = jnp.dot(block_read, block_write.T, preferred_element_type=jnp.float32)
        weights = decay_mat * scores[:, :, None] * block_step[None, :, :]
        local_part = jnp.einsum("tsh,shp->thp", weights, block_x, precision=highest)
        kept = ((block_turn == block_turn[0]) & jnp.logical_not(block_start[0])).astype(jnp.float32)
        inner = running - offset
        read_f = block_read.astype(jnp.float32)
        projected = jnp.einsum("hpn,tn->thp", state_now, read_f, precision=highest)
        since = inner + kept[:, None] * since_now[None, :]
        carry_factor = jnp.exp(inner) * kept[:, None]
        output = (
            local_part
            + carry_factor[:, :, None] * projected
            + jnp.exp(since)[:, :, None] * block_begin
            + skip_value[None, :, None] * block_x
        )
        last_weights = decay_mat[-1] * block_step
        new_state = carry_factor[-1][:, None, None] * state_now + jnp.einsum(
            "sh,shp,sn->hpn",
            last_weights,
            block_x,
            block_write.astype(jnp.float32),
            precision=highest,
        )
        return ((new_state, since[-1]), output)

    start_state = (
        jnp.zeros((head_count, head_dim, state_dim), jnp.float32),
        jnp.zeros((head_count,), jnp.float32),
    )
    final_state, outputs = lax.scan(advance, start_state, blocked)
    mixed = outputs.reshape(row_count, head_count, head_dim)
    gate_f = gate_values.astype(jnp.float32).reshape(row_count, head_count, head_dim)
    gated_out = mixed * jax.nn.silu(gate_f)
    mean_square = jnp.mean(gated_out * gated_out, axis=-1, keepdims=True)
    normed = (
        gated_out * lax.rsqrt(mean_square + 1e-05) * gain_value.reshape(head_count, head_dim)[None]
    )
    return normed.reshape(row_count, head_count * head_dim)


def learner(
    inputs,
    start_read,
    step_bias,
    rate_log,
    skip_gain,
    norm_gain,
    gate_values,
    write_proj,
    read_proj,
    step_raw,
    turn_index,
    cotangent,
):

    def forward(input_value, read_value, bias_value, rate_value, skip_value, gain_value):
        return mixer(
            input_value,
            read_value,
            bias_value,
            rate_value,
            skip_value,
            gain_value,
            gate_values,
            write_proj,
            read_proj,
            step_raw,
            turn_index,
        )

    primal, pullback = jax.vjp(
        forward,
        inputs.astype(jnp.float32),
        start_read.astype(jnp.float32),
        step_bias,
        rate_log,
        skip_gain,
        norm_gain,
    )
    return pullback(cotangent.astype(jnp.float32))


def local(
    inputs,
    gate_values,
    write_proj,
    read_proj,
    step_raw,
    cotangent,
    step_bias,
    rate_log,
    skip_gain,
    norm_gain,
    state_bank,
    turn_index,
    turn_slot,
):
    devices = lax.axis_size("dp")
    inverse = jnp.argsort(turn_slot)
    head_part = state_bank.shape[1]
    row_count = inputs.shape[0]
    position = lax.axis_index("dp")
    moved_inputs, moved_gates, moved_cot, moved_steps = (
        lax.all_to_all(inputs, "dp", split_axis=1, concat_axis=0, tiled=True),
        lax.all_to_all(gate_values, "dp", split_axis=1, concat_axis=0, tiled=True),
        lax.all_to_all(cotangent, "dp", split_axis=1, concat_axis=0, tiled=True),
        lax.all_to_all(step_raw, "dp", split_axis=1, concat_axis=0, tiled=True),
    )
    write_all, read_all = (
        lax.all_gather(write_proj, "dp", axis=0, tiled=True),
        lax.all_gather(read_proj, "dp", axis=0, tiled=True),
    )
    turns_all = lax.all_gather(turn_index, "dp", axis=0, tiled=True)
    start_head = position * head_part
    own_bias = lax.dynamic_slice_in_dim(step_bias, start_head, head_part)
    own_rate = lax.dynamic_slice_in_dim(rate_log, start_head, head_part)
    own_skip = lax.dynamic_slice_in_dim(skip_gain, start_head, head_part)
    own_gain = lax.dynamic_slice_in_dim(norm_gain, start_head * HDIM, head_part * HDIM)
    initial = state_bank[turn_slot].reshape(devices, TMAX, head_part, HDIM, DSTATE)

    def split_rows(value):
        return value.reshape((devices, row_count) + value.shape[1:])

    read_split = split_rows(read_all)
    turns_split = split_rows(turns_all)
    start_read = jax.vmap(project_turns)(initial, read_split, turns_split)
    batched = jax.vmap(learner, in_axes=(0, 0, None, None, None, None, 0, 0, 0, 0, 0, 0))
    gradients = batched(
        split_rows(moved_inputs),
        start_read,
        own_bias,
        own_rate,
        own_skip,
        own_gain,
        split_rows(moved_gates),
        split_rows(write_all),
        read_split,
        split_rows(moved_steps),
        turns_split,
        split_rows(moved_cot),
    )
    grad_local = gradients[0].reshape(devices * row_count, head_part * HDIM).astype(jnp.bfloat16)
    grad_inputs = lax.all_to_all(grad_local, "dp", split_axis=0, concat_axis=1, tiled=True)
    read_grad = gradients[1].astype(jnp.bfloat16)
    holder_turns = jax.vmap(turn_grads, in_axes=(0, 0, 0, None))(
        read_grad, read_split, turns_split, TMAX
    )
    state_grad = holder_turns.reshape(devices * TMAX, head_part, HDIM, DSTATE).astype(jnp.bfloat16)[
        inverse
    ]
    own_heads = jnp.stack(
        [
            jnp.sum(gradients[2], axis=0),
            jnp.sum(gradients[3], axis=0),
            jnp.sum(gradients[4], axis=0),
        ]
    )
    head_grads = lax.all_gather(own_heads, "dp", axis=1, tiled=True)
    gain_grad = jnp.sum(gradients[5], axis=0)
    return (grad_inputs, state_grad, gain_grad, head_grads)


def solution(mesh):
    in_specs = (
        P(("groups", "dp"), None),
        P(("groups", "dp"), None),
        P(("groups", "dp"), None),
        P(("groups", "dp"), None),
        P(("groups", "dp"), None),
        P(("groups", "dp"), None),
        P(),
        P(),
        P(),
        P(),
        P("groups", "dp", None, None),
        P(("groups", "dp")),
        P("groups"),
    )
    out_specs = (
        P(("groups", "dp"), None),
        P("groups", "dp", None, None),
        P(("groups", "dp")),
        P("groups", None),
    )
    return jax.shard_map(local, mesh=mesh, in_specs=in_specs, out_specs=out_specs, check_vma=False)
```

profile of v0, /device:TPU:9, one launch (start us, length us, event | category | flops | bytes accessed | tf_op | source)
XLA Modules:
  0.0 391.7 jit_solution(12096214340189381911)
XLA Ops:
  7.2 1.4 all_to_all.54
  8.6 6.6 %all-to-all-start = ((bf16[256,16,4]{0,2,1:T(4,128)(2,1)}), bf16[256,16,4]{0,2,1:T(4,128)(2,1)S(1)}, u32[]{:S(2)}, u32[]{:S(2)}) async-start(bf16[256,16,4]{0,2,1:T(4,128)(2,1)} %all_to_all.54), calls=%async_computation | async-start | bytes 65536 | tf_op jit(solution)/shard_map/all_to_all | solution.py:185
  15.1 4.1 %copy.107 = bf16[256,4096]{0,1:T(8,128)(2,1)} copy(bf16[256,4096]{1,0:T(8,128)(2,1)} %param.14) | data formatting | bytes 4194304 | tf_op jit(solution)/shard_map/all_to_all | solution.py:183
  19.2 1.0 all-to-all-done
  20.2 5.2 %all-to-all-start.3 = ((bf16[256,16,256]{0,2,1:T(8,128)(2,1)}), bf16[256,16,256]{0,2,1:T(8,128)(2,1)S(1)}, u32[]{:S(2)}, u32[]{:S(2)}) async-start(bf16[256,16,256]{0,2,1:T(8,128)(2,1)} %bitcast.249), calls=%async_computation.3 | async-start | bytes 4194304 | tf_op jit(solution)/shard_map/all_to_all | solution.py:183
  25.4 0.7 all-gather.7.cloned.1.call-update
  26.2 4.1 %copy.106 = bf16[256,4096]{0,1:T(8,128)(2,1)} copy(bf16[256,4096]{1,0:T(8,128)(2,1)} %param.13) | data formatting | bytes 4194304 | tf_op jit(solution)/shard_map/all_to_all | solution.py:182
  30.3 46.6 %all-to-all-done.3 = bf16[256,16,256]{0,2,1:T(8,128)(2,1)S(1)} async-done(((bf16[256,16,256]{0,2,1:T(8,128)(2,1)}), bf16[256,16,256]{0,2,1:T(8,128)(2,1)S(1)}, u32[]{:S(2)}, u32[]{:S(2)}) %all-to-all-start.3) | async-done | bytes 2097184 | tf_op jit(solution)/shard_map/all_to_all | solution.py:183
  76.9 6.9 %all-to-all-start.2 = ((bf16[256,16,256]{0,2,1:T(8,128)(2,1)}), bf16[256,16,256]{0,2,1:T(8,128)(2,1)}, u32[]{:S(2)}, u32[]{:S(2)}) async-start(bf16[256,16,256]{0,2,1:T(8,128)(2,1)} %bitcast.247), calls=%async_computation.2 | async-start | bytes 4194304 | tf_op jit(solution)/shard_map/all_to_all | solution.py:182
  83.8 0.7 all-gather.5.cloned.1.call-update
  84.6 63.3 %all-gather = s32[16,1,256]{2,1,0:T(1,128)S(1)} all-gather(s32[1,1,256]{2,1,0:T(1,128)S(1)} %bitcast.271), channel_id=1, replica_groups=mesh['groups'=2,'dp'=16] {'dp'}, dimensions={0}, use_global_device_ids=true | all-gather | bytes 17408 | tf_op jit(solution)/shard_map/all_gather | solution.py:191
  147.8 0.1 dynamic_slice.103
  147.9 0.6 dynamic_slice.104
  148.5 0.8 dynamic_slice.105
  149.3 0.1 mul.487
  149.4 4.1 %copy.105 = bf16[256,4096]{0,1:T(8,128)(2,1)} copy(bf16[256,4096]{1,0:T(8,128)(2,1)} %param.18) | data formatting | bytes 4194304 | tf_op jit(solution)/shard_map/all_to_all | solution.py:184
  153.4 5.3 %gather_fusion = bf16[64,4,64,128]{3,2,1,0:T(8,128)(2,1)} fusion(bf16[64,4,64,128]{3,2,1,0:T(8,128)(2,1)} %param.23, s32[1024]{0:T(1024)S(1)} %pad_clamp_fusion.1), kind=kCustom, calls=%fused_computation | custom fusion | bytes 8388864 | tf_op jit(solution)/shard_map/gather | solution.py:197
  158.7 0.6 fusion.96
  159.4 0.9 compare_and_fusion
  160.3 0.2 fusion.69
  160.5 2.3 reduce-window.26
  162.8 0.2 slice_reduce_fusion.1
  163.0 0.1 broadcast_add_fusion.1
  163.3 4.9 %fusion.64 = f32[16,4,64,256]{3,2,1,0:T(8,128)} fusion(bf16[16,256,128,1]{2,1,3,0:T(8,128)(2,1)} %bitcast.253), kind=kOutput, calls=%fused_computation.90 | convolution fusion | flops 1610612736 | bytes 5242880 | tf_op jit(solution)/shard_map/vmap(jvp())/while/body/eval_jaxpr/hpn,tn->thp/dot_general | solution.py:85
  168.2 4.3 %fusion.99 = f32[16,256,256]{2,1,0:T(8,128)} fusion(bf16[16,256,128]{2,1,0:T(8,128)(2,1)} %bitcast.254, bf16[16,256,128]{2,1,0:T(8,128)(2,1)} %bitcast.257), kind=kOutput, calls=%fused_computation.162 | convolution fusion | flops 268435456 | bytes 6291456 | tf_op jit(solution)/shard_map/vmap(jvp())/while/body/eval_jaxpr/dot_general | solution.py:79
  172.6 5.7 %bitcast_convert_fusion = bf16[16,256,4,64]{1,3,2,0:T(8,128)(2,1)} fusion(bf16[16,4,4,64,128]{4,3,2,1,0:T(8,128)(2,1)S(1)} %bitcast.252, pred[16,256,4]{1,2,0:T(4,128)(4,1)S(1)} %iota_compare_fusion.1, bf16[16,256,128]{2,1,0:T(8,128)(2,1)S(1)} %bitcast.255), kind=kOutput, calls=%fused_computation.52 | convolution fusion | flops 1076887552 | bytes 7356416 | tf_op jit(solution)/shard_map/vmap(tgn,ghpn->thp)/dot_general | solution.py:16
  178.3 2.4 convert_element_type.148
  180.7 4.0 %all-to-all-start.1 = ((bf16[256,16,256]{0,2,1:T(8,128)(2,1)}), bf16[256,16,256]{0,2,1:T(8,128)(2,1)S(1)}, u32[]{:S(2)}, u32[]{:S(2)}) async-start(bf16[256,16,256]{0,2,1:T(8,128)(2,1)} %bitcast.248), calls=%async_computation.1 | async-start | bytes 4194304 | tf_op jit(solution)/shard_map/all_to_all | solution.py:184
  184.7 6.2 %fusion.48 = (f32[16,256,4]{1,2,0:T(4,128)S(1)}, f32[16,4,64,256]{3,2,1,0:T(8,128)}) fusion(bf16[256,16,256]{0,2,1:T(8,128)(2,1)} %all-to-all-done.2, bf16[16,256,128,1]{2,1,3,0:T(8,128)(2,1)} %bitcast.258), kind=kOutput, calls=%fused_computation.73 | convolution fusion | flops 1613742080 | bytes 7405568 | tf_op jit(solution)/shard_map/vmap(transpose(jvp()))/while/body/eval_jaxpr/sh,shp,sn->hpn/dot_general | solution.py:95
  191.0 0.8 multiply_bitcast_fusion
  191.8 2.4 select_reduce_fusion
  194.2 2.1 bitcast_convert_fusion.1
  196.3 16.8 %multiply_reduce_fusion.2 = (f32[16,256,4]{1,2,0:T(4,128)S(1)}, f32[16,256,4,64]{1,3,2,0:T(8,128)}, f32[16,256,4,64]{1,3,2,0:T(8,128)}) fusion(f32[16,256,4,64]{1,3,2,0:T(8,128)S(1)} %bitcast.250, f32[16,256,4,64]{1,3,2,0:T(8,128)S(1)} %bitcast.251, f32[4]{0:T(128)S(1)} %copy-done.36, bf16[16,256,4,64]{1,3,2,0:T(8,128)(2,1)S(1)} %copy-done.12, ...), kind=kOutput, calls=%fused_computation.78 | convolution fusion | flops 3252666368 | bytes 30736400 | tf_op jit(solution)/shard_map/vmap(jvp())/while/body/eval_jaxpr/tsh,shp->thp/dot_general | solution.py:81
  213.2 5.9 %fusion.2 = f32[16,256,4]{1,2,0:T(4,128)} fusion(f32[16,256,4]{1,2,0:T(4,128)S(1)} %select_reduce_fusion, f32[16,256,4]{1,2,0:T(4,128)S(1)} %get-tuple-element.439, pred[16,256,256]{2,1,0:T(8,128)(4,1)S(1)} %compare_and_fusion), kind=kLoop, calls=%fused_computation.6 | loop fusion | flops 16760832 | bytes 1245184 | tf_op jit(solution)/shard_map/vmap(jvp())/while/body/eval_jaxpr/reduce_sum | solution.py:78
  219.1 11.7 %all-to-all-done.1 = bf16[256,16,256]{0,2,1:T(8,128)(2,1)S(1)} async-done(((bf16[256,16,256]{0,2,1:T(8,128)(2,1)}), bf16[256,16,256]{0,2,1:T(8,128)(2,1)S(1)}, u32[]{:S(2)}, u32[]{:S(2)}) %all-to-all-start.1) | async-done | bytes 2097184 | tf_op jit(solution)/shard_map/all_to_all | solution.py:184
  230.8 0.4 convert_element_type.147
  231.2 1.7 copy-done.2
  233.0 2.4 multiply_reduce_fusion
  235.4 0.9 multiply_multiply_fusion
  236.5 3.8 fusion.46
  240.4 28.3 %fusion.28 = (f32[16,256,4]{1,2,0:T(4,128)S(1)}, f32[16,256,4]{1,2,0:T(4,128)S(1)}, f32[16,256,4]{1,2,0:T(4,128)}, f32[16,256,4]{1,2,0:T(4,128)S(1)}, f32[16,256,256,4]{2,1,3,0:T(8,128)}) fusion(f32[16,256,4]{1,2,0:T(4,128)S(1)} %bitcast.261, f32[16,256,256]{2,1,0:T(8,128)S(1)} %copy-done.7, f32[16,256,4]{1,2,0:T(4,128)S(1)} %copy-done.23, ...), kind=kOutput, calls=%fused_computation.42 | convolution fusion | flops 3292463104 | bytes 28966912 | tf_op jit(solution)/shard_map/vmap(transpose(jvp()))/while/body/eval_jaxpr/tsh,shp->thp/dot_general | solution.py:81
  268.7 0.6 copy-done.21
  269.4 0.1 bitcast_add_fusion.2
  269.5 9.9 %reduce-window.28 = f32[16,4,2,128]{3,0,1,2:T(8,128)S(1)} reduce-window(f32[16,4,2,128]{3,0,1,2:T(8,128)S(1)} %copy.91, f32[]{:T(128)} %constant.180.clone.1), window={size=1x1x1x128 pad=0_0x0_0x0_0x0_127}, to_apply=%region_14.15 | reduce-window | flops 2080768 | bytes 131076 | tf_op jit(solution)/shard_map/reduce-window
  279.5 0.1 slice_reduce_fusion
  279.6 0.1 broadcast_add_fusion
  279.8 1.1 slice.63
  280.9 1.9 fusion.86
  282.8 19.1 %fusion.38 = bf16[16,256,4,64]{1,3,2,0:T(8,128)(2,1)} fusion(f32[16,4,64,256]{3,2,1,0:T(8,128)} %get-tuple-element.442, f32[16,256,4,64]{1,3,2,0:T(8,128)} %copy-done.5, f32[4]{0:T(128)} %dynamic_slice.104, f32[16,256,4]{1,2,0:T(4,128)S(1)} %get-tuple-element.437, f32[16,256,4]{1,2,0:T(4,128)} %copy-done.22, f32[16,256,256]{2,1,0:T(8,128)} %fusion.99, ...), kind=kOutput, calls=%fused_computation.57 | convolution fusion | flops 3243245568 | bytes 15925264 | tf_op jit(solution)/shard_map/vmap(transpose(jvp()))/while/body/eval_jaxpr/tsh,shp->thp/dot_general | solution.py:81
  301.9 6.3 %all-to-all-start.4 = ((bf16[16,256,256]{1,2,0:T(8,128)(2,1)}), bf16[16,256,256]{1,2,0:T(8,128)(2,1)}, u32[]{:S(2)}, u32[]{:S(2)}) async-start(bf16[16,256,256]{1,2,0:T(8,128)(2,1)} %bitcast.259), calls=%async_computation.4 | async-start | bytes 4194304 | tf_op jit(solution)/shard_map/all_to_all | solution.py:221
  308.2 2.0 sort.17
  310.3 5.0 %fusion.37 = f32[256]{0:T(256)S(1)} fusion(f32[16,256,4,64]{1,3,2,0:T(8,128)} %get-tuple-element.443, f32[256]{0:T(256)S(1)} %dynamic_slice.105, f32[16,256,4]{1,2,0:T(4,128)S(1)} %multiply_multiply_fusion, f32[16,256,4]{1,2,0:T(4,128)S(1)} %fusion.87, bf16[256,16,256]{0,2,1:T(8,128)(2,1)} %all-to-all-done.2, bf16[256,16,256]{0,2,1:T(8,128)(2,1)} %copy-done, ...), kind=kLoop, calls=%fused_computation.51 | loop fusion | flops 16776960 | bytes 10618880 | tf_op jit(solution)/shard_map/reduce_sum | solution.py:233
  315.2 0.1 reduce_sum.242
  315.3 0.1 reduce_sum.256
  315.4 0.1 copy.93
  315.5 0.2 multiply_reduce_fusion.4
  315.7 0.1 copy.94
  315.8 50.2 %all-gather.1 = f32[16,4,3]{2,1,0:T(4,128)S(1)} all-gather(f32[1,4,3]{2,1,0:T(4,128)S(1)} %bitcast.266), channel_id=1, replica_groups=mesh['groups'=2,'dp'=16] {'dp'}, dimensions={0}, use_global_device_ids=true | all-gather | bytes 816 | tf_op jit(solution)/shard_map/all_gather | solution.py:236
  366.0 0.7 copy.95
  366.7 5.3 %convert_bitcast_fusion = bf16[16,4,4,64,128]{4,3,1,2,0:T(8,128)(2,1)S(1)} fusion(pred[16,256,4]{1,2,0:T(4,128)(4,1)S(1)} %copy-done.25, f32[16,256,4,64]{1,3,2,0:T(8,128)} %copy-done.5, bf16[16,256,128]{2,1,0:T(8,128)(2,1)S(1)} %bitcast.256, f32[16,256,4]{1,2,0:T(4,128)S(1)} %copy-done.19), kind=kOutput, calls=%fused_computation.75 | convolution fusion | flops 1080033280 | bytes 9519104 | tf_op jit(solution)/shard_map/vmap(tgn,thp->ghpn)/dot_general | solution.py:24
  371.9 2.9 copy.89
  374.8 0.6 reduce_sum.215
  375.5 5.3 %gather_fusion.1 = bf16[64,4,64,128]{3,2,1,0:T(8,128)(2,1)} fusion(bf16[64,4,64,128]{3,2,1,0:T(8,128)(2,1)} %bitcast.246, s32[1024]{0:T(1024)S(1)} %pad_clamp_fusion), kind=kCustom, calls=%fused_computation.1 | custom fusion | bytes 8388864 | tf_op jit(solution)/shard_map/gather | solution.py:226
  380.8 4.1 %copy.108 = bf16[256,4096]{1,0:T(8,128)(2,1)} copy(bf16[256,4096]{0,1:T(8,128)(2,1)} %bitcast.33) | data formatting | bytes 4194304 | tf_op jit(solution)/shard_map/all_to_all | solution.py:221
  (103 shorter events, 0.9 us)
Async XLA Ops:
  8.6 11.6 %all-to-all-start = ((bf16[256,16,4]{0,2,1:T(4,128)(2,1)}), bf16[256,16,4]{0,2,1:T(4,128)(2,1)S(1)}, u32[]{:S(2)}, u32[]{:S(2)}) async-start(bf16[256,16,4]{0,2,1:T(4,128)(2,1)} %all_to_all.54), calls=%async_computation | async-start | bytes 65536 | tf_op jit(solution)/shard_map/all_to_all | solution.py:185
  20.2 170.8 %copy-start.14 = (bf16[256,16,4]{0,2,1:T(4,128)(2,1)}, bf16[256,16,4]{0,2,1:T(4,128)(2,1)S(1)}, u32[]{:S(2)}) copy-start(bf16[256,16,4]{0,2,1:T(4,128)(2,1)S(1)} %all-to-all-done) | copy-start | bytes 98308
  20.2 56.7 %all-to-all-start.3 = ((bf16[256,16,256]{0,2,1:T(8,128)(2,1)}), bf16[256,16,256]{0,2,1:T(8,128)(2,1)S(1)}, u32[]{:S(2)}, u32[]{:S(2)}) async-start(bf16[256,16,256]{0,2,1:T(8,128)(2,1)} %bitcast.249), calls=%async_computation.3 | async-start | bytes 4194304 | tf_op jit(solution)/shard_map/all_to_all | solution.py:183
  25.4 137.9 %all-gather.7.cloned.1.call-start = ((), (), s32[]{:S(2)}) async-start(), calls=%async_computation.6 | async-start | bytes 1114112 | tf_op jit(solution)/shard_map/all_gather | solution.py:189
  26.1 58.4 %copy-start.34 = (s32[64]{0:T(128)S(1)}, s32[64]{0:T(128)}, u32[]{:S(2)}) copy-start(s32[64]{0:T(128)} %param.25) | copy-start | bytes 772
  26.1 58.4 %copy-start.30 = (s32[256]{0:T(256)S(1)}, s32[256]{0:T(256)}, u32[]{:S(2)}) copy-start(s32[256]{0:T(256)} %param.24) | copy-start | bytes 3076
  26.2 121.7 %copy-start.32 = (f32[64]{0:T(128)S(1)}, f32[64]{0:T(128)}, u32[]{:S(2)}) copy-start(f32[64]{0:T(128)} %param.19) | copy-start | bytes 772
  26.2 121.8 %copy-start.33 = (f32[64]{0:T(128)S(1)}, f32[64]{0:T(128)}, u32[]{:S(2)}) copy-start(f32[64]{0:T(128)} %param.21) | copy-start | bytes 772
  76.9 101.4 %copy-start = (bf16[256,16,256]{0,2,1:T(8,128)(2,1)}, bf16[256,16,256]{0,2,1:T(8,128)(2,1)S(1)}, u32[]{:S(2)}) copy-start(bf16[256,16,256]{0,2,1:T(8,128)(2,1)S(1)} %all-to-all-done.3) | copy-start | bytes 6291460
  76.9 103.8 %all-to-all-start.2 = ((bf16[256,16,256]{0,2,1:T(8,128)(2,1)}), bf16[256,16,256]{0,2,1:T(8,128)(2,1)}, u32[]{:S(2)}, u32[]{:S(2)}) async-start(bf16[256,16,256]{0,2,1:T(8,128)(2,1)} %bitcast.247), calls=%async_computation.2 | async-start | bytes 4194304 | tf_op jit(solution)/shard_map/all_to_all | solution.py:182
  83.8 84.4 %all-gather.5.cloned.1.call-start = ((), (), s32[]{:S(2)}) async-start(), calls=%async_computation.5 | async-start | bytes 1114112 | tf_op jit(solution)/shard_map/all_gather | solution.py:188
  147.9 43.0 %copy-start.27 = (f32[4]{0:T(128)}, f32[4]{0:T(128)S(1)}, u32[]{:S(2)}) copy-start(f32[4]{0:T(128)S(1)} %dynamic_slice.103) | copy-start | bytes 52
  153.4 5.3 %copy-start.31 = (f32[64]{0:T(128)S(1)}, f32[64]{0:T(128)}, u32[]{:S(2)}) copy-start(f32[64]{0:T(128)} %param.20) | copy-start | bytes 772
  159.4 13.2 %copy-start.24 = (pred[16,256,4]{1,2,0:T(4,128)(4,1)}, pred[16,256,4]{1,2,0:T(4,128)(4,1)S(1)}, u32[]{:S(2)}) copy-start(pred[16,256,4]{1,2,0:T(4,128)(4,1)S(1)} %iota_compare_fusion.1) | copy-start | bytes 49156
  168.2 4.3 %copy-start.9 = (bf16[64,4,64,128]{3,2,1,0:T(8,128)(2,1)S(1)}, bf16[64,4,64,128]{3,2,1,0:T(8,128)(2,1)}, u32[]{:S(2)}) copy-start(bf16[64,4,64,128]{3,2,1,0:T(8,128)(2,1)} %gather_fusion) | copy-start | bytes 12582916
  168.2 4.3 %copy-start.10 = (bf16[4096,128]{1,0:T(8,128)(2,1)S(1)}, bf16[4096,128]{1,0:T(8,128)(2,1)}, u32[]{:S(2)}) copy-start(bf16[4096,128]{1,0:T(8,128)(2,1)} %all-gather.7.cloned.1.call-done) | copy-start | bytes 3145732
  180.7 50.1 %all-to-all-start.1 = ((bf16[256,16,256]{0,2,1:T(8,128)(2,1)}), bf16[256,16,256]{0,2,1:T(8,128)(2,1)S(1)}, u32[]{:S(2)}, u32[]{:S(2)}) async-start(bf16[256,16,256]{0,2,1:T(8,128)(2,1)} %bitcast.248), calls=%async_computation.1 | async-start | bytes 4194304 | tf_op jit(solution)/shard_map/all_to_all | solution.py:184
  184.7 11.6 %copy-start.6 = (f32[16,256,256]{2,1,0:T(8,128)S(1)}, f32[16,256,256]{2,1,0:T(8,128)}, u32[]{:S(2)}) copy-start(f32[16,256,256]{2,1,0:T(8,128)} %fusion.99) | copy-start | bytes 12582916
  184.7 11.6 %copy-start.8 = (f32[256,16,256]{0,2,1:T(8,128)S(1)}, f32[256,16,256]{0,2,1:T(8,128)}, u32[]{:S(2)}) copy-start(f32[256,16,256]{0,2,1:T(8,128)} %convert_element_type.148) | copy-start | bytes 12582916
  190.9 5.4 %copy-start.3 = (f32[16,4,64,256]{3,2,1,0:T(8,128)S(1)}, f32[16,4,64,256]{3,2,1,0:T(8,128)}, u32[]{:S(2)}) copy-start(f32[16,4,64,256]{3,2,1,0:T(8,128)} %fusion.64) | copy-start | bytes 12582916
  190.9 5.4 %copy-start.12 = (bf16[16,256,4,64]{1,3,2,0:T(8,128)(2,1)S(1)}, bf16[16,256,4,64]{1,3,2,0:T(8,128)(2,1)}, u32[]{:S(2)}) copy-start(bf16[16,256,4,64]{1,3,2,0:T(8,128)(2,1)} %bitcast_convert_fusion) | copy-start | bytes 6291460
  190.9 5.4 %copy-start.36 = (f32[4]{0:T(128)S(1)}, f32[4]{0:T(128)}, u32[]{:S(2)}) copy-start(f32[4]{0:T(128)} %dynamic_slice.104) | copy-start | bytes 52
  191.8 21.4 %copy-start.22 = (f32[16,256,4]{1,2,0:T(4,128)}, f32[16,256,4]{1,2,0:T(4,128)S(1)}, u32[]{:S(2)}) copy-start(f32[16,256,4]{1,2,0:T(4,128)S(1)} %get-tuple-element.440) | copy-start | bytes 196612
  194.2 19.0 %copy-start.17 = (f32[16,256,4]{1,2,0:T(4,128)}, f32[16,256,4]{1,2,0:T(4,128)S(1)}, u32[]{:S(2)}) copy-start(f32[16,256,4]{1,2,0:T(4,128)S(1)} %get-tuple-element.433) | copy-start | bytes 196612
  213.2 22.2 %copy-start.16 = (f32[16,256,4]{1,2,0:T(4,128)}, f32[16,256,4]{1,2,0:T(4,128)S(1)}, u32[]{:S(2)}) copy-start(f32[16,256,4]{1,2,0:T(4,128)S(1)} %get-tuple-element.430) | copy-start | bytes 196612
  230.8 2.2 copy-start.2
  233.0 3.4 copy-start.20
  233.0 3.5 copy-start.1
  233.0 3.5 copy-start.4
  233.0 3.5 copy-start.13
  236.4 3.9 copy-start.15
  236.5 3.9 copy-start.18
  236.5 3.9 %copy-start.7 = (f32[16,256,256]{2,1,0:T(8,128)S(1)}, f32[16,256,256]{2,1,0:T(8,128)}, u32[]{:S(2)}) copy-start(f32[16,256,256]{2,1,0:T(8,128)} %fusion.99) | copy-start | bytes 12582916
  236.5 3.9 %copy-start.23 = (f32[16,256,4]{1,2,0:T(4,128)S(1)}, f32[16,256,4]{1,2,0:T(4,128)}, u32[]{:S(2)}) copy-start(f32[16,256,4]{1,2,0:T(4,128)} %copy-done.22) | copy-start | bytes 196612
  240.3 28.4 %copy-start.5 = (f32[16,256,4,64]{1,3,2,0:T(8,128)}, f32[16,256,4,64]{1,3,2,0:T(8,128)S(1)}, u32[]{:S(2)}) copy-start(f32[16,256,4,64]{1,3,2,0:T(8,128)S(1)} %get-tuple-element.429) | copy-start | bytes 12582916
  268.7 0.6 copy-start.21
  301.9 6.3 %copy-start.35 = (s32[64]{0:T(128)S(1)}, s32[64]{0:T(128)}, u32[]{:S(2)}) copy-start(s32[64]{0:T(128)} %param.25) | copy-start | bytes 772
  301.9 78.8 %all-to-all-start.4 = ((bf16[16,256,256]{1,2,0:T(8,128)(2,1)}), bf16[16,256,256]{1,2,0:T(8,128)(2,1)}, u32[]{:S(2)}, u32[]{:S(2)}) async-start(bf16[16,256,256]{1,2,0:T(8,128)(2,1)} %bitcast.259), calls=%async_computation.4 | async-start | bytes 4194304 | tf_op jit(solution)/shard_map/all_to_all | solution.py:221
  310.2 5.3 %copy-start.29 = (f32[4]{0:T(128)S(1)}, f32[4]{0:T(128)}, u32[]{:S(2)}) copy-start(f32[4]{0:T(128)} %get-tuple-element.435) | copy-start | bytes 52
  310.2 5.5 %copy-start.28 = (f32[4]{0:T(128)S(1)}, f32[4]{0:T(128)}, u32[]{:S(2)}) copy-start(f32[4]{0:T(128)} %get-tuple-element.427) | copy-start | bytes 52
  310.3 56.4 %copy-start.11 = (bf16[4096,128]{1,0:T(8,128)(2,1)S(1)}, bf16[4096,128]{1,0:T(8,128)(2,1)}, u32[]{:S(2)}) copy-start(bf16[4096,128]{1,0:T(8,128)(2,1)} %all-gather.7.cloned.1.call-done) | copy-start | bytes 3145732
  310.3 56.4 %copy-start.19 = (f32[16,256,4]{1,2,0:T(4,128)S(1)}, f32[16,256,4]{1,2,0:T(4,128)}, u32[]{:S(2)}) copy-start(f32[16,256,4]{1,2,0:T(4,128)} %copy-done.17) | copy-start | bytes 196612
  310.3 56.4 %copy-start.25 = (pred[16,256,4]{1,2,0:T(4,128)(4,1)S(1)}, pred[16,256,4]{1,2,0:T(4,128)(4,1)}, u32[]{:S(2)}) copy-start(pred[16,256,4]{1,2,0:T(4,128)(4,1)} %copy-done.24) | copy-start | bytes 49156
  371.9 2.9 copy-start.26
Sparse Core Ops, SparseCore 0:
  28.4 51.8 all-gather.6
  86.8 51.8 all-gather.4
where the time goes:
time: 393 us; the launch traced here: 392 us
  blocking collectives  113 us (29%)
  matrix products  90.7 us (23%)
  waiting for transfers between devices  60.7 us (15%)
  other arithmetic  44.7 us (11%)
  local copies, waits for them, and re-layouts  38.5 us (10%)
  starting transfers between devices  29 us (7%)
  between operations  14.7 us (4%)
    dot_general x3, matrix products, advance(): local_part = jnp.einsum('tsh,shp->thp', weights, block_x, precision=highest)  64.2 us
    all_gather x1, blocking collectives, local(): turns_all = lax.all_gather(turn_index, 'dp', axis=0, tiled=True)  63.3 us
    all_gather x1, blocking collectives, local(): head_grads = lax.all_gather(own_heads, 'dp', axis=1, tiled=True)  50.2 us
    all_to_all x1, waiting for transfers between devices, local(): lax.all_to_all(gate_values, 'dp', split_axis=1, concat_axis=0, tiled=True)  46.6 us
    another operation x5, other arithmetic  12.3 us
    all_to_all x1, waiting for transfers between devices, local(): lax.all_to_all(cotangent, 'dp', split_axis=1, concat_axis=0, tiled=True)  11.7 us
  transfers between devices with their start and end apart: 7, of which 3 were waited for; matrix products, arithmetic and copies ran while one was open for 25% of the time, Pallas kernels for 0%

commit v1 on v0

--- a/solution.py
+++ b/solution.py
@@ -188,7 +188,31 @@
         lax.all_gather(write_proj, "dp", axis=0, tiled=True),
         lax.all_gather(read_proj, "dp", axis=0, tiled=True),
     )
-    turns_all = lax.all_gather(turn_index, "dp", axis=0, tiled=True)
+    reached, plain, vec_out = (lax.axis_size("dp"), lax.axis_index("dp"), turn_index.shape[0])
+    turns_all = lax.dynamic_update_slice_in_dim(
+        jnp.zeros(
+            [idx * reached if pp == 0 else idx for pp, idx in enumerate(turn_index.shape)],
+            turn_index.dtype,
+        ),
+        turn_index,
+        plain * vec_out,
+        axis=0,
+    )
+    kept_arr = mixed_arr = turn_index
+    it = 1
+    while it < reached // 2 + 1:
+        kept_arr = lax.ppermute(kept_arr, "dp", [(pp, (pp + 1) % reached) for pp in range(reached)])
+        turns_all = lax.dynamic_update_slice_in_dim(
+            turns_all, kept_arr, (plain - it) % reached * vec_out, axis=0
+        )
+        if 2 * it < reached:
+            mixed_arr = lax.ppermute(
+                mixed_arr, "dp", [(pp, (pp - 1) % reached) for pp in range(reached)]
+            )
+            turns_all = lax.dynamic_update_slice_in_dim(
+                turns_all, mixed_arr, (plain + it) % reached * vec_out, axis=0
+            )
+        it += 1
     start_head = position * head_part
     own_bias = lax.dynamic_slice_in_dim(step_bias, start_head, head_part)
     own_rate = lax.dynamic_slice_in_dim(rate_log, start_head, head_part)

time: 393 us -> 413 us (1.051)
  starting transfers between devices: 29 us -> 95.9 us
  blocking collectives: 113 us -> 50.2 us
  waiting for transfers between devices: 60.7 us -> 69.2 us
    all_gather x1 -> x0, blocking collectives: 63.3 us -> none  [local(): turns_all = lax.all_gather(turn_index, 'dp', axis=0, tiled=True)]
    ppermute x0 -> x15, starting transfers between devices: none -> 62.2 us  [the longest x8 34.8 us: local(): lax.ppermute(kept_arr, 'dp', [(pp, (pp + 1) % reached) for pp in range(re...]
    ppermute x0 -> x15, waiting for transfers between devices: none -> 9.36 us  [the longest x8 7.93 us: local(): lax.ppermute(kept_arr, 'dp', [(pp, (pp + 1) % reached) for pp in range(re...]
    all_to_all x1, starting transfers between devices: 3.99 us -> 8.7 us  [local(): lax.all_to_all(cotangent, 'dp', split_axis=1, concat_axis=0, tiled=True)]
  transfers between devices with their start and end apart: 7 -> 22, of which waited for: 3 -> 13; matrix products, arithmetic and copies ran while one was open for 25% -> 25% of each run, Pallas kernels for 0% -> 0%
where the time goes in v1:
time: 413 us; the launch traced here: 408 us
  starting transfers between devices  95.9 us (23%)
  matrix products  90.8 us (22%)
  waiting for transfers between devices  69.2 us (17%)
  blocking collectives  50.2 us (12%)
  other arithmetic  44.6 us (11%)
  local copies, waits for them, and re-layouts  42.3 us (10%)
  between operations  15 us (4%)
    dot_general x3, matrix products, advance(): local_part = jnp.einsum('tsh,shp->thp', weights, block_x, precision=highest)  64.3 us
    all_gather x1, blocking collectives, local(): head_grads = lax.all_gather(own_heads, 'dp', axis=1, tiled=True)  50.2 us
    all_to_all x1, waiting for transfers between devices, local(): lax.all_to_all(gate_values, 'dp', split_axis=1, concat_axis=0, tiled=True)  46.6 us
    ppermute x8, starting transfers between devices, local(): lax.ppermute(kept_arr, 'dp', [(pp, (pp + 1) % reached) for pp in range(re...  34.8 us
    ppermute x7, starting transfers between devices, local(): lax.ppermute(mixed_arr, 'dp', [(pp, (pp - 1) % reached) for pp in range(r...  27.4 us
    another operation x5, other arithmetic  12.3 us
    all_to_all x1, waiting for transfers between devices, local(): lax.all_to_all(cotangent, 'dp', split_axis=1, concat_axis=0, tiled=True)  11.6 us
    all_to_all x1, starting transfers between devices, local(): lax.all_to_all(cotangent, 'dp', split_axis=1, concat_axis=0, tiled=True)  8.7 us
  transfers between devices with their start and end apart: 22, of which 13 were waited for; matrix products, arithmetic and copies ran while one was open for 25% of the time, Pallas kernels for 0%

profile of v1, /device:TPU:9, one launch (start us, length us, event | category | flops | bytes accessed | tf_op | source)
XLA Modules:
  0.0 407.9 jit_solution(7416059005860521515)
XLA Ops:
  7.2 1.4 all_to_all.54
  8.6 6.6 %all-to-all-start = ((bf16[256,16,4]{0,2,1:T(4,128)(2,1)}), bf16[256,16,4]{0,2,1:T(4,128)(2,1)S(1)}, u32[]{:S(2)}, u32[]{:S(2)}) async-start(bf16[256,16,4]{0,2,1:T(4,128)(2,1)} %all_to_all.54), calls=%async_computation | async-start | bytes 65536 | tf_op jit(solution)/shard_map/all_to_all | solution.py:185
  15.1 4.1 copy.107
  19.2 1.0 all-to-all-done
  20.2 5.2 %all-to-all-start.3 = ((bf16[256,16,256]{0,2,1:T(8,128)(2,1)}), bf16[256,16,256]{0,2,1:T(8,128)(2,1)S(1)}, u32[]{:S(2)}, u32[]{:S(2)}) async-start(bf16[256,16,256]{0,2,1:T(8,128)(2,1)} %bitcast.245), calls=%async_computation.3 | async-start | bytes 4194304 | tf_op jit(solution)/shard_map/all_to_all | solution.py:183
  25.4 0.7 all-gather.6.cloned.1.call-update
  26.2 4.1 %copy.106 = bf16[256,4096]{0,1:T(8,128)(2,1)} copy(bf16[256,4096]{1,0:T(8,128)(2,1)} %param.13) | data formatting | bytes 4194304 | tf_op jit(solution)/shard_map/all_to_all | solution.py:182
  30.3 46.6 %all-to-all-done.3 = bf16[256,16,256]{0,2,1:T(8,128)(2,1)S(1)} async-done(((bf16[256,16,256]{0,2,1:T(8,128)(2,1)}), bf16[256,16,256]{0,2,1:T(8,128)(2,1)S(1)}, u32[]{:S(2)}, u32[]{:S(2)}) %all-to-all-start.3) | async-done | bytes 2097184 | tf_op jit(solution)/shard_map/all_to_all | solution.py:183
  76.9 6.9 %all-to-all-start.2 = ((bf16[256,16,256]{0,2,1:T(8,128)(2,1)}), bf16[256,16,256]{0,2,1:T(8,128)(2,1)}, u32[]{:S(2)}, u32[]{:S(2)}) async-start(bf16[256,16,256]{0,2,1:T(8,128)(2,1)} %bitcast.243), calls=%async_computation.2 | async-start | bytes 4194304 | tf_op jit(solution)/shard_map/all_to_all | solution.py:182
  83.8 1.5 collective-permute-start
  85.4 0.6 fusion.96
  86.1 6.4 %collective-permute-done = s32[256]{0:T(256)S(1)} collective-permute-done((s32[256]{0:T(256)S(1)}, s32[256]{0:T(256)S(1)}, u32[]{:S(2)}, u32[]{:S(2)}) %collective-permute-start) | collective-permute-done | bytes 1056 | tf_op jit(solution)/shard_map/ppermute | solution.py:204
  92.5 2.4 collective-permute-start.2
  95.0 27.4 %collective-permute-start.3 = (s32[256]{0:T(256)S(1)}, s32[256]{0:T(256)S(1)}, u32[]{:S(2)}, u32[]{:S(2)}) collective-permute-start(s32[256]{0:T(256)S(1)} %collective-permute-done.1), channel_id=1, source_target_pairs={{0,15},{1,0},{2,1},{3,2},{4,3},{5,4},{6,5},{7,6},{8,7},{9,8},{10,9... | collective-permute-start | bytes 3080 | tf_op jit(solution)/shard_map/ppermute | solution.py:209
  122.4 0.6 collective-permute-done.2
  123.0 14.4 %collective-permute-start.4 = (s32[256]{0:T(256)S(1)}, s32[256]{0:T(256)S(1)}, u32[]{:S(2)}, u32[]{:S(2)}) collective-permute-start(s32[256]{0:T(256)S(1)} %collective-permute-done.2), channel_id=1, source_target_pairs={{0,1},{1,2},{2,3},{3,4},{4,5},{5,6},{6,7},{7,8},{8,9},{9,10},{10,1... | collective-permute-start | bytes 3080 | tf_op jit(solution)/shard_map/ppermute | solution.py:204
  137.4 0.4 collective-permute-done.3
  138.1 3.5 collective-permute-start.6
  141.7 0.4 collective-permute-done.5
  142.4 3.2 collective-permute-start.8
  145.6 0.4 collective-permute-done.7
  146.0 0.3 collective-permute-done.8
  146.3 3.2 collective-permute-start.10
  149.6 0.6 dynamic_slice.104
  150.2 3.2 collective-permute-start.12
  153.6 0.8 dynamic_slice.105
  154.4 4.1 %copy.105 = bf16[256,4096]{0,1:T(8,128)(2,1)} copy(bf16[256,4096]{1,0:T(8,128)(2,1)} %param.18) | data formatting | bytes 4194304 | tf_op jit(solution)/shard_map/all_to_all | solution.py:184
  158.5 3.4 collective-permute-start.14
  161.9 5.3 %gather_fusion = bf16[64,4,64,128]{3,2,1,0:T(8,128)(2,1)} fusion(bf16[64,4,64,128]{3,2,1,0:T(8,128)(2,1)} %param.23, s32[1024]{0:T(1024)S(1)} %pad_clamp_fusion.1), kind=kCustom, calls=%fused_computation | custom fusion | bytes 8388864 | tf_op jit(solution)/shard_map/gather | solution.py:221
  170.8 0.9 compare_and_fusion
  172.0 2.3 reduce-window.26
  174.7 5.0 %fusion.64 = f32[16,4,64,256]{3,2,1,0:T(8,128)} fusion(bf16[16,256,128,1]{2,1,3,0:T(8,128)(2,1)} %bitcast.249), kind=kOutput, calls=%fused_computation.90 | convolution fusion | flops 1610612736 | bytes 5242880 | tf_op jit(solution)/shard_map/vmap(jvp())/while/body/eval_jaxpr/hpn,tn->thp/dot_general | solution.py:85
  179.7 4.3 %fusion.99 = f32[16,256,256]{2,1,0:T(8,128)} fusion(bf16[16,256,128]{2,1,0:T(8,128)(2,1)} %bitcast.250, bf16[16,256,128]{2,1,0:T(8,128)(2,1)} %bitcast.253), kind=kOutput, calls=%fused_computation.161 | convolution fusion | flops 268435456 | bytes 6291456 | tf_op jit(solution)/shard_map/vmap(jvp())/while/body/eval_jaxpr/dot_general | solution.py:79
  184.0 5.7 %bitcast_convert_fusion = bf16[16,256,4,64]{1,3,2,0:T(8,128)(2,1)} fusion(bf16[16,4,4,64,128]{4,3,2,1,0:T(8,128)(2,1)S(1)} %bitcast.248, pred[16,256,4]{1,2,0:T(4,128)(4,1)S(1)} %iota_compare_fusion.1, bf16[16,256,128]{2,1,0:T(8,128)(2,1)S(1)} %bitcast.251), kind=kOutput, calls=%fused_computation.52 | convolution fusion | flops 1076887552 | bytes 7356416 | tf_op jit(solution)/shard_map/vmap(tgn,ghpn->thp)/dot_general | solution.py:16
  189.7 2.4 convert_element_type.148
  192.2 8.7 %all-to-all-start.1 = ((bf16[256,16,256]{0,2,1:T(8,128)(2,1)}), bf16[256,16,256]{0,2,1:T(8,128)(2,1)S(1)}, u32[]{:S(2)}, u32[]{:S(2)}) async-start(bf16[256,16,256]{0,2,1:T(8,128)(2,1)} %bitcast.244), calls=%async_computation.1 | async-start | bytes 4194304 | tf_op jit(solution)/shard_map/all_to_all | solution.py:184
  200.9 6.2 %fusion.48 = (f32[16,256,4]{1,2,0:T(4,128)S(1)}, f32[16,4,64,256]{3,2,1,0:T(8,128)}) fusion(bf16[256,16,256]{0,2,1:T(8,128)(2,1)} %all-to-all-done.2, bf16[16,256,128,1]{2,1,3,0:T(8,128)(2,1)} %bitcast.254), kind=kOutput, calls=%fused_computation.73 | convolution fusion | flops 1613742080 | bytes 7405568 | tf_op jit(solution)/shard_map/vmap(transpose(jvp()))/while/body/eval_jaxpr/sh,shp,sn->hpn/dot_general | solution.py:95
  207.1 0.8 multiply_bitcast_fusion
  207.9 2.4 select_reduce_fusion
  210.4 2.1 bitcast_convert_fusion.1
  212.5 16.9 %multiply_reduce_fusion.2 = (f32[16,256,4]{1,2,0:T(4,128)S(1)}, f32[16,256,4,64]{1,3,2,0:T(8,128)}, f32[16,256,4,64]{1,3,2,0:T(8,128)}) fusion(f32[16,256,4,64]{1,3,2,0:T(8,128)S(1)} %bitcast.246, f32[16,256,4,64]{1,3,2,0:T(8,128)S(1)} %bitcast.247, f32[4]{0:T(128)S(1)} %copy-done.36, bf16[16,256,4,64]{1,3,2,0:T(8,128)(2,1)S(1)} %copy-done.12, ...), kind=kOutput, calls=%fused_computation.78 | convolution fusion | flops 3252666368 | bytes 30736400 | tf_op jit(solution)/shard_map/vmap(jvp())/while/body/eval_jaxpr/tsh,shp->thp/dot_general | solution.py:81
  229.4 5.8 %fusion.2 = f32[16,256,4]{1,2,0:T(4,128)} fusion(f32[16,256,4]{1,2,0:T(4,128)S(1)} %select_reduce_fusion, f32[16,256,4]{1,2,0:T(4,128)S(1)} %get-tuple-element.439, pred[16,256,256]{2,1,0:T(8,128)(4,1)S(1)} %compare_and_fusion), kind=kLoop, calls=%fused_computation.6 | loop fusion | flops 16760832 | bytes 1245184 | tf_op jit(solution)/shard_map/vmap(jvp())/while/body/eval_jaxpr/reduce_sum | solution.py:78
  235.3 11.6 %all-to-all-done.1 = bf16[256,16,256]{0,2,1:T(8,128)(2,1)S(1)} async-done(((bf16[256,16,256]{0,2,1:T(8,128)(2,1)}), bf16[256,16,256]{0,2,1:T(8,128)(2,1)S(1)}, u32[]{:S(2)}, u32[]{:S(2)}) %all-to-all-start.1) | async-done | bytes 2097184 | tf_op jit(solution)/shard_map/all_to_all | solution.py:184
  246.9 0.4 convert_element_type.147
  247.3 1.7 copy-done.2
  249.1 2.4 multiply_reduce_fusion
  251.4 1.0 multiply_multiply_fusion
  252.6 3.8 fusion.46
  256.5 28.3 %fusion.28 = (f32[16,256,4]{1,2,0:T(4,128)S(1)}, f32[16,256,4]{1,2,0:T(4,128)S(1)}, f32[16,256,4]{1,2,0:T(4,128)}, f32[16,256,4]{1,2,0:T(4,128)S(1)}, f32[16,256,256,4]{2,1,3,0:T(8,128)}) fusion(f32[16,256,4]{1,2,0:T(4,128)S(1)} %bitcast.257, f32[16,256,256]{2,1,0:T(8,128)S(1)} %copy-done.7, f32[16,256,4]{1,2,0:T(4,128)S(1)} %copy-done.23, ...), kind=kOutput, calls=%fused_computation.42 | convolution fusion | flops 3292463104 | bytes 28966912 | tf_op jit(solution)/shard_map/vmap(transpose(jvp()))/while/body/eval_jaxpr/tsh,shp->thp/dot_general | solution.py:81
  284.8 0.6 copy-done.21
  285.6 9.9 %reduce-window.28 = f32[16,4,2,128]{3,0,1,2:T(8,128)S(1)} reduce-window(f32[16,4,2,128]{3,0,1,2:T(8,128)S(1)} %copy.91, f32[]{:T(128)} %constant.263.clone.1), window={size=1x1x1x128 pad=0_0x0_0x0_0x0_127}, to_apply=%region_14.15 | reduce-window | flops 2080768 | bytes 131076 | tf_op jit(solution)/shard_map/reduce-window
  295.9 1.1 slice.63
  297.0 1.8 fusion.86
  298.8 19.1 %fusion.38 = bf16[16,256,4,64]{1,3,2,0:T(8,128)(2,1)} fusion(f32[16,4,64,256]{3,2,1,0:T(8,128)} %get-tuple-element.442, f32[16,256,4,64]{1,3,2,0:T(8,128)} %copy-done.5, f32[4]{0:T(128)} %dynamic_slice.104, f32[16,256,4]{1,2,0:T(4,128)S(1)} %get-tuple-element.437, f32[16,256,4]{1,2,0:T(4,128)} %copy-done.22, f32[16,256,256]{2,1,0:T(8,128)} %fusion.99, ...), kind=kOutput, calls=%fused_computation.57 | convolution fusion | flops 3243245568 | bytes 15925264 | tf_op jit(solution)/shard_map/vmap(transpose(jvp()))/while/body/eval_jaxpr/tsh,shp->thp/dot_general | solution.py:81
  318.0 6.2 %all-to-all-start.4 = ((bf16[16,256,256]{1,2,0:T(8,128)(2,1)}), bf16[16,256,256]{1,2,0:T(8,128)(2,1)}, u32[]{:S(2)}, u32[]{:S(2)}) async-start(bf16[16,256,256]{1,2,0:T(8,128)(2,1)} %bitcast.255), calls=%async_computation.4 | async-start | bytes 4194304 | tf_op jit(solution)/shard_map/all_to_all | solution.py:245
  324.2 2.0 sort.17
  326.3 5.0 %fusion.37 = f32[256]{0:T(256)S(1)} fusion(f32[16,256,4,64]{1,3,2,0:T(8,128)} %get-tuple-element.443, f32[256]{0:T(256)S(1)} %dynamic_slice.105, f32[16,256,4]{1,2,0:T(4,128)S(1)} %multiply_multiply_fusion, f32[16,256,4]{1,2,0:T(4,128)S(1)} %fusion.87, bf16[256,16,256]{0,2,1:T(8,128)(2,1)} %all-to-all-done.2, bf16[256,16,256]{0,2,1:T(8,128)(2,1)} %copy-done, ...), kind=kLoop, calls=%fused_computation.51 | loop fusion | flops 16776960 | bytes 10618880 | tf_op jit(solution)/shard_map/reduce_sum | solution.py:257
  331.9 50.2 %all-gather = f32[16,4,3]{2,1,0:T(4,128)S(1)} all-gather(f32[1,4,3]{2,1,0:T(4,128)S(1)} %bitcast.260), channel_id=1, replica_groups=mesh['groups'=2,'dp'=16] {'dp'}, dimensions={0}, use_global_device_ids=true | all-gather | bytes 816 | tf_op jit(solution)/shard_map/all_gather | solution.py:260
  382.0 0.7 copy.95
  382.7 5.3 %convert_bitcast_fusion = bf16[16,4,4,64,128]{4,3,1,2,0:T(8,128)(2,1)S(1)} fusion(pred[16,256,4]{1,2,0:T(4,128)(4,1)S(1)} %copy-done.25, f32[16,256,4,64]{1,3,2,0:T(8,128)} %copy-done.5, bf16[16,256,128]{2,1,0:T(8,128)(2,1)S(1)} %bitcast.252, f32[16,256,4]{1,2,0:T(4,128)S(1)} %copy-done.19), kind=kOutput, calls=%fused_computation.75 | convolution fusion | flops 1080033280 | bytes 9519104 | tf_op jit(solution)/shard_map/vmap(tgn,thp->ghpn)/dot_general | solution.py:24
  388.0 2.9 copy.89
  390.9 0.6 reduce_sum.215
  391.5 5.3 %gather_fusion.1 = bf16[64,4,64,128]{3,2,1,0:T(8,128)(2,1)} fusion(bf16[64,4,64,128]{3,2,1,0:T(8,128)(2,1)} %bitcast.242, s32[1024]{0:T(1024)S(1)} %pad_clamp_fusion), kind=kCustom, calls=%fused_computation.1 | custom fusion | bytes 8388864 | tf_op jit(solution)/shard_map/gather | solution.py:250
  396.8 4.1 copy.108
  (149 shorter events, 6.8 us)
Async XLA Ops:
  8.6 11.6 %all-to-all-start = ((bf16[256,16,4]{0,2,1:T(4,128)(2,1)}), bf16[256,16,4]{0,2,1:T(4,128)(2,1)S(1)}, u32[]{:S(2)}, u32[]{:S(2)}) async-start(bf16[256,16,4]{0,2,1:T(4,128)(2,1)} %all_to_all.54), calls=%async_computation | async-start | bytes 65536 | tf_op jit(solution)/shard_map/all_to_all | solution.py:185
  20.2 187.0 %copy-start.14 = (bf16[256,16,4]{0,2,1:T(4,128)(2,1)}, bf16[256,16,4]{0,2,1:T(4,128)(2,1)S(1)}, u32[]{:S(2)}) copy-start(bf16[256,16,4]{0,2,1:T(4,128)(2,1)S(1)} %all-to-all-done) | copy-start | bytes 98308
  20.2 56.7 %all-to-all-start.3 = ((bf16[256,16,256]{0,2,1:T(8,128)(2,1)}), bf16[256,16,256]{0,2,1:T(8,128)(2,1)S(1)}, u32[]{:S(2)}, u32[]{:S(2)}) async-start(bf16[256,16,256]{0,2,1:T(8,128)(2,1)} %bitcast.245), calls=%async_computation.3 | async-start | bytes 4194304 | tf_op jit(solution)/shard_map/all_to_all | solution.py:183
  25.4 149.3 %all-gather.6.cloned.1.call-start = ((), (), s32[]{:S(2)}) async-start(), calls=%async_computation.6 | async-start | bytes 1114112 | tf_op jit(solution)/shard_map/all_gather | solution.py:189
  26.1 57.7 %copy-start.30 = (s32[256]{0:T(256)S(1)}, s32[256]{0:T(256)}, u32[]{:S(2)}) copy-start(s32[256]{0:T(256)} %param.24) | copy-start | bytes 3076
  26.1 59.3 %copy-start.34 = (s32[64]{0:T(128)S(1)}, s32[64]{0:T(128)}, u32[]{:S(2)}) copy-start(s32[64]{0:T(128)} %param.25) | copy-start | bytes 772
  26.2 59.3 %copy-start.31 = (f32[64]{0:T(128)S(1)}, f32[64]{0:T(128)}, u32[]{:S(2)}) copy-start(f32[64]{0:T(128)} %param.20) | copy-start | bytes 772
  26.2 123.3 %copy-start.32 = (f32[64]{0:T(128)S(1)}, f32[64]{0:T(128)}, u32[]{:S(2)}) copy-start(f32[64]{0:T(128)} %param.19) | copy-start | bytes 772
  26.2 123.4 %copy-start.33 = (f32[64]{0:T(128)S(1)}, f32[64]{0:T(128)}, u32[]{:S(2)}) copy-start(f32[64]{0:T(128)} %param.21) | copy-start | bytes 772
  76.9 112.9 %copy-start = (bf16[256,16,256]{0,2,1:T(8,128)(2,1)}, bf16[256,16,256]{0,2,1:T(8,128)(2,1)S(1)}, u32[]{:S(2)}) copy-start(bf16[256,16,256]{0,2,1:T(8,128)(2,1)S(1)} %all-to-all-done.3) | copy-start | bytes 6291460
  76.9 115.3 %all-to-all-start.2 = ((bf16[256,16,256]{0,2,1:T(8,128)(2,1)}), bf16[256,16,256]{0,2,1:T(8,128)(2,1)}, u32[]{:S(2)}, u32[]{:S(2)}) async-start(bf16[256,16,256]{0,2,1:T(8,128)(2,1)} %bitcast.243), calls=%async_computation.2 | async-start | bytes 4194304 | tf_op jit(solution)/shard_map/all_to_all | solution.py:182
  83.8 95.9 %all-gather.4.cloned.1.call-start = ((), (), s32[]{:S(2)}) async-start(), calls=%async_computation.5 | async-start | bytes 1114112 | tf_op jit(solution)/shard_map/all_gather | solution.py:188
  83.8 8.6 %collective-permute-start = (s32[256]{0:T(256)S(1)}, s32[256]{0:T(256)S(1)}, u32[]{:S(2)}, u32[]{:S(2)}) collective-permute-start(s32[256]{0:T(256)S(1)} %copy-done.30), channel_id=1, source_target_pairs={{0,1},{1,2},{2,3},{3,4},{4,5},{5,6},{6,7},{7,8},{8,9},{9,10},{10,1... | collective-permute-start | bytes 3080 | tf_op jit(solution)/shard_map/ppermute | solution.py:204
  85.4 9.6 %collective-permute-start.1 = (s32[256]{0:T(256)S(1)}, s32[256]{0:T(256)S(1)}, u32[]{:S(2)}, u32[]{:S(2)}) collective-permute-start(s32[256]{0:T(256)S(1)} %copy-done.30), channel_id=1, source_target_pairs={{0,15},{1,0},{2,1},{3,2},{4,3},{5,4},{6,5},{7,6},{8,7},{9,8},{10,9... | collective-permute-start | bytes 3080 | tf_op jit(solution)/shard_map/ppermute | solution.py:209
  92.5 30.6 %collective-permute-start.2 = (s32[256]{0:T(256)S(1)}, s32[256]{0:T(256)S(1)}, u32[]{:S(2)}, u32[]{:S(2)}) collective-permute-start(s32[256]{0:T(256)S(1)} %collective-permute-done), channel_id=1, source_target_pairs={{0,1},{1,2},{2,3},{3,4},{4,5},{5,6},{6,7},{7,8},{8,9},{9,10},{10,1... | collective-permute-start | bytes 3080 | tf_op jit(solution)/shard_map/ppermute | solution.py:204
  95.0 42.9 %collective-permute-start.3 = (s32[256]{0:T(256)S(1)}, s32[256]{0:T(256)S(1)}, u32[]{:S(2)}, u32[]{:S(2)}) collective-permute-start(s32[256]{0:T(256)S(1)} %collective-permute-done.1), channel_id=1, source_target_pairs={{0,15},{1,0},{2,1},{3,2},{4,3},{5,4},{6,5},{7,6},{8,7},{9,8},{10,9... | collective-permute-start | bytes 3080 | tf_op jit(solution)/shard_map/ppermute | solution.py:209
  123.0 15.1 %collective-permute-start.4 = (s32[256]{0:T(256)S(1)}, s32[256]{0:T(256)S(1)}, u32[]{:S(2)}, u32[]{:S(2)}) collective-permute-start(s32[256]{0:T(256)S(1)} %collective-permute-done.2), channel_id=1, source_target_pairs={{0,1},{1,2},{2,3},{3,4},{4,5},{5,6},{6,7},{7,8},{8,9},{9,10},{10,1... | collective-permute-start | bytes 3080 | tf_op jit(solution)/shard_map/ppermute | solution.py:204
  137.9 4.3 %collective-permute-start.5 = (s32[256]{0:T(256)S(1)}, s32[256]{0:T(256)S(1)}, u32[]{:S(2)}, u32[]{:S(2)}) collective-permute-start(s32[256]{0:T(256)S(1)} %collective-permute-done.3), channel_id=1, source_target_pairs={{0,15},{1,0},{2,1},{3,2},{4,3},{5,4},{6,5},{7,6},{8,7},{9,8},{10,9... | collective-permute-start | bytes 3080 | tf_op jit(solution)/shard_map/ppermute | solution.py:209
  138.1 4.3 %collective-permute-start.6 = (s32[256]{0:T(256)S(1)}, s32[256]{0:T(256)S(1)}, u32[]{:S(2)}, u32[]{:S(2)}) collective-permute-start(s32[256]{0:T(256)S(1)} %collective-permute-done.4), channel_id=1, source_target_pairs={{0,1},{1,2},{2,3},{3,4},{4,5},{5,6},{6,7},{7,8},{8,9},{9,10},{10,1... | collective-permute-start | bytes 3080 | tf_op jit(solution)/shard_map/ppermute | solution.py:204
  142.1 3.9 collective-permute-start.7
  142.4 3.9 collective-permute-start.8
  146.0 4.1 %collective-permute-start.9 = (s32[256]{0:T(256)S(1)}, s32[256]{0:T(256)S(1)}, u32[]{:S(2)}, u32[]{:S(2)}) collective-permute-start(s32[256]{0:T(256)S(1)} %collective-permute-done.7), channel_id=1, source_target_pairs={{0,15},{1,0},{2,1},{3,2},{4,3},{5,4},{6,5},{7,6},{8,7},{9,8},{10,9... | collective-permute-start | bytes 3080 | tf_op jit(solution)/shard_map/ppermute | solution.py:209
  146.3 3.9 collective-permute-start.10
  149.5 57.6 %copy-start.27 = (f32[4]{0:T(128)}, f32[4]{0:T(128)S(1)}, u32[]{:S(2)}) copy-start(f32[4]{0:T(128)S(1)} %dynamic_slice.103) | copy-start | bytes 52
  150.1 8.3 %collective-permute-start.11 = (s32[256]{0:T(256)S(1)}, s32[256]{0:T(256)S(1)}, u32[]{:S(2)}, u32[]{:S(2)}) collective-permute-start(s32[256]{0:T(256)S(1)} %collective-permute-done.9), channel_id=1, source_target_pairs={{0,15},{1,0},{2,1},{3,2},{4,3},{5,4},{6,5},{7,6},{8,7},{9,8},{10,9... | collective-permute-start | bytes 3080 | tf_op jit(solution)/shard_map/ppermute | solution.py:209
  150.2 8.3 %collective-permute-start.12 = (s32[256]{0:T(256)S(1)}, s32[256]{0:T(256)S(1)}, u32[]{:S(2)}, u32[]{:S(2)}) collective-permute-start(s32[256]{0:T(256)S(1)} %collective-permute-done.10), channel_id=1, source_target_pairs={{0,1},{1,2},{2,3},{3,4},{4,5},{5,6},{6,7},{7,8},{8,9},{9,10},{10,1... | collective-permute-start | bytes 3080 | tf_op jit(solution)/shard_map/ppermute | solution.py:204
  158.5 11.9 %collective-permute-start.13 = (s32[256]{0:T(256)S(1)}, s32[256]{0:T(256)S(1)}, u32[]{:S(2)}, u32[]{:S(2)}) collective-permute-start(s32[256]{0:T(256)S(1)} %collective-permute-done.11), channel_id=1, source_target_pairs={{0,15},{1,0},{2,1},{3,2},{4,3},{5,4},{6,5},{7,6},{8,7},{9,8},{10,9... | collective-permute-start | bytes 3080 | tf_op jit(solution)/shard_map/ppermute | solution.py:209
  158.5 12.1 %collective-permute-start.14 = (s32[256]{0:T(256)S(1)}, s32[256]{0:T(256)S(1)}, u32[]{:S(2)}, u32[]{:S(2)}) collective-permute-start(s32[256]{0:T(256)S(1)} %collective-permute-done.12), channel_id=1, source_target_pairs={{0,1},{1,2},{2,3},{3,4},{4,5},{5,6},{6,7},{7,8},{8,9},{9,10},{10,1... | collective-permute-start | bytes 3080 | tf_op jit(solution)/shard_map/ppermute | solution.py:204
  170.8 13.2 %copy-start.24 = (pred[16,256,4]{1,2,0:T(4,128)(4,1)}, pred[16,256,4]{1,2,0:T(4,128)(4,1)S(1)}, u32[]{:S(2)}) copy-start(pred[16,256,4]{1,2,0:T(4,128)(4,1)S(1)} %iota_compare_fusion.1) | copy-start | bytes 49156
  179.7 4.3 %copy-start.9 = (bf16[64,4,64,128]{3,2,1,0:T(8,128)(2,1)S(1)}, bf16[64,4,64,128]{3,2,1,0:T(8,128)(2,1)}, u32[]{:S(2)}) copy-start(bf16[64,4,64,128]{3,2,1,0:T(8,128)(2,1)} %gather_fusion) | copy-start | bytes 12582916
  179.7 4.3 %copy-start.10 = (bf16[4096,128]{1,0:T(8,128)(2,1)S(1)}, bf16[4096,128]{1,0:T(8,128)(2,1)}, u32[]{:S(2)}) copy-start(bf16[4096,128]{1,0:T(8,128)(2,1)} %all-gather.6.cloned.1.call-done) | copy-start | bytes 3145732
  192.2 54.7 %all-to-all-start.1 = ((bf16[256,16,256]{0,2,1:T(8,128)(2,1)}), bf16[256,16,256]{0,2,1:T(8,128)(2,1)S(1)}, u32[]{:S(2)}, u32[]{:S(2)}) async-start(bf16[256,16,256]{0,2,1:T(8,128)(2,1)} %bitcast.244), calls=%async_computation.1 | async-start | bytes 4194304 | tf_op jit(solution)/shard_map/all_to_all | solution.py:184
  200.9 11.6 %copy-start.6 = (f32[16,256,256]{2,1,0:T(8,128)S(1)}, f32[16,256,256]{2,1,0:T(8,128)}, u32[]{:S(2)}) copy-start(f32[16,256,256]{2,1,0:T(8,128)} %fusion.99) | copy-start | bytes 12582916
  200.9 11.6 %copy-start.8 = (f32[256,16,256]{0,2,1:T(8,128)S(1)}, f32[256,16,256]{0,2,1:T(8,128)}, u32[]{:S(2)}) copy-start(f32[256,16,256]{0,2,1:T(8,128)} %convert_element_type.148) | copy-start | bytes 12582916
  207.1 5.4 %copy-start.3 = (f32[16,4,64,256]{3,2,1,0:T(8,128)S(1)}, f32[16,4,64,256]{3,2,1,0:T(8,128)}, u32[]{:S(2)}) copy-start(f32[16,4,64,256]{3,2,1,0:T(8,128)} %fusion.64) | copy-start | bytes 12582916
  207.1 5.4 %copy-start.12 = (bf16[16,256,4,64]{1,3,2,0:T(8,128)(2,1)S(1)}, bf16[16,256,4,64]{1,3,2,0:T(8,128)(2,1)}, u32[]{:S(2)}) copy-start(bf16[16,256,4,64]{1,3,2,0:T(8,128)(2,1)} %bitcast_convert_fusion) | copy-start | bytes 6291460
  207.1 5.4 %copy-start.36 = (f32[4]{0:T(128)S(1)}, f32[4]{0:T(128)}, u32[]{:S(2)}) copy-start(f32[4]{0:T(128)} %dynamic_slice.104) | copy-start | bytes 52
  207.9 21.4 %copy-start.22 = (f32[16,256,4]{1,2,0:T(4,128)}, f32[16,256,4]{1,2,0:T(4,128)S(1)}, u32[]{:S(2)}) copy-start(f32[16,256,4]{1,2,0:T(4,128)S(1)} %get-tuple-element.440) | copy-start | bytes 196612
  210.4 19.0 %copy-start.17 = (f32[16,256,4]{1,2,0:T(4,128)}, f32[16,256,4]{1,2,0:T(4,128)S(1)}, u32[]{:S(2)}) copy-start(f32[16,256,4]{1,2,0:T(4,128)S(1)} %get-tuple-element.433) | copy-start | bytes 196612
  229.4 22.0 %copy-start.16 = (f32[16,256,4]{1,2,0:T(4,128)}, f32[16,256,4]{1,2,0:T(4,128)S(1)}, u32[]{:S(2)}) copy-start(f32[16,256,4]{1,2,0:T(4,128)S(1)} %get-tuple-element.430) | copy-start | bytes 196612
  246.9 2.2 copy-start.2
  249.0 3.4 copy-start.20
  249.0 3.4 copy-start.1
  249.0 3.5 copy-start.4
  249.0 3.5 copy-start.13
  252.5 3.9 copy-start.15
  252.5 3.9 copy-start.18
  252.5 3.9 copy-start.7
  252.6 3.9 copy-start.23
  256.4 28.4 %copy-start.5 = (f32[16,256,4,64]{1,3,2,0:T(8,128)}, f32[16,256,4,64]{1,3,2,0:T(8,128)S(1)}, u32[]{:S(2)}) copy-start(f32[16,256,4,64]{1,3,2,0:T(8,128)S(1)} %get-tuple-element.429) | copy-start | bytes 12582916
  284.8 0.6 copy-start.21
  318.0 6.3 %copy-start.35 = (s32[64]{0:T(128)S(1)}, s32[64]{0:T(128)}, u32[]{:S(2)}) copy-start(s32[64]{0:T(128)} %param.25) | copy-start | bytes 772
  318.0 78.9 %all-to-all-start.4 = ((bf16[16,256,256]{1,2,0:T(8,128)(2,1)}), bf16[16,256,256]{1,2,0:T(8,128)(2,1)}, u32[]{:S(2)}, u32[]{:S(2)}) async-start(bf16[16,256,256]{1,2,0:T(8,128)(2,1)} %bitcast.255), calls=%async_computation.4 | async-start | bytes 4194304 | tf_op jit(solution)/shard_map/all_to_all | solution.py:245
  326.3 5.3 %copy-start.29 = (f32[4]{0:T(128)S(1)}, f32[4]{0:T(128)}, u32[]{:S(2)}) copy-start(f32[4]{0:T(128)} %get-tuple-element.435) | copy-start | bytes 52
  326.3 5.5 %copy-start.28 = (f32[4]{0:T(128)S(1)}, f32[4]{0:T(128)}, u32[]{:S(2)}) copy-start(f32[4]{0:T(128)} %get-tuple-element.427) | copy-start | bytes 52
  326.3 56.4 %copy-start.11 = (bf16[4096,128]{1,0:T(8,128)(2,1)S(1)}, bf16[4096,128]{1,0:T(8,128)(2,1)}, u32[]{:S(2)}) copy-start(bf16[4096,128]{1,0:T(8,128)(2,1)} %all-gather.6.cloned.1.call-done) | copy-start | bytes 3145732
  326.3 56.4 %copy-start.19 = (f32[16,256,4]{1,2,0:T(4,128)S(1)}, f32[16,256,4]{1,2,0:T(4,128)}, u32[]{:S(2)}) copy-start(f32[16,256,4]{1,2,0:T(4,128)} %copy-done.17) | copy-start | bytes 196612
  326.3 56.4 %copy-start.25 = (pred[16,256,4]{1,2,0:T(4,128)(4,1)S(1)}, pred[16,256,4]{1,2,0:T(4,128)(4,1)}, u32[]{:S(2)}) copy-start(pred[16,256,4]{1,2,0:T(4,128)(4,1)} %copy-done.24) | copy-start | bytes 49156
  388.0 2.9 copy-start.26
Sparse Core Ops, SparseCore 0:
  28.4 51.8 all-gather.5
  86.8 51.8 all-gather.3
